TPU v7x, 128 devices: a whole 4x4x4 slice. The times are simulated.
128 devices in a mesh: prow: 4 (over x), pcol: 32 (over y, z, core).
Axes of the slice: x: 4, y: 4, z: 4, core: 2. Of those that a mesh axis runs over, the one named last changes fastest.
Arguments:
- matrix: float32 [128, 4, 128, 1, 32, 128], P(None, 'prow', None, None, 'pcol')
- pivots: int32 [128], replicated, may hold values from 0 to 65535, as said below
Outputs:
- factored: float32 [128, 4, 128, 1, 32, 128], P(None, 'prow', None, None, 'pcol')
Inputs may be any that keep to these rules, and one draw needn't show every extreme that they name: `pivots`: entry j lies between j and 65535; the last entry is 65535.
All inputs are finite; a program needn't handle non-finite values.
Results may differ from a plain program's by a relative error of at most 0.0001.
Values sent between devices are 32-bit elements; how exact they have to be, the bound alone decides.
A program may use at most 128 MiB of HBM per device.

v0:
```python
import jax
import jax.numpy as jnp
from jax import lax
from jax.sharding import PartitionSpec as P


def from_root(value, axis, source):
    kept = jnp.where(lax.axis_index(axis) == source, value, 0).astype(value.dtype)
    return lax.psum(kept, axis)


def eliminate(square):
    size = square.shape[0]
    positions = jnp.arange(size, dtype=jnp.int32)

    def reduce_step(column_no, factors):
        column = factors[:, column_no]
        pivot_value = factors[column_no, column_no]
        below = positions > column_no
        multiplier = jnp.where(below, column / pivot_value, 0.0)
        pivot_row = jnp.where(below, factors[column_no], 0.0)
        factors = factors - multiplier[:, None] * pivot_row[None, :]
        return jnp.where(
            below[:, None] & (positions[None, :] == column_no), multiplier[:, None], factors
        )

    return lax.fori_loop(0, size, reduce_step, square)


def both_inverses(packed):
    size = packed.shape[0]
    positions = jnp.arange(size, dtype=jnp.int32)
    strict_low = jnp.where(positions[:, None] > positions[None, :], packed, 0.0)
    strict_up = jnp.where(positions[:, None] < positions[None, :], packed, 0.0)
    diag_values = jnp.sum(jnp.where(positions[:, None] == positions[None, :], packed, 0.0), axis=1)

    def row_step(step_no, inverses):
        upper_inv, lower_inv = inverses
        low_no = jnp.asarray(step_no).astype(jnp.int32)
        up_no = (size - 1 - jnp.asarray(step_no)).astype(jnp.int32)
        low_row = lax.dynamic_index_in_dim(strict_low, low_no, 0, keepdims=False)
        up_row = lax.dynamic_index_in_dim(strict_up, up_no, 0, keepdims=False)
        pivot_value = lax.dynamic_index_in_dim(diag_values, up_no, 0, keepdims=False)
        low_unit = (positions == low_no).astype(jnp.float32)
        up_unit = (positions == up_no).astype(jnp.float32)
        new_low = low_unit - jnp.dot(
            low_row, lower_inv, precision=lax.Precision.HIGHEST, preferred_element_type=jnp.float32
        )
        new_up = (
            up_unit
            - jnp.dot(
                up_row,
                upper_inv,
                precision=lax.Precision.HIGHEST,
                preferred_element_type=jnp.float32,
            )
        ) / pivot_value
        lower_inv = lax.dynamic_update_index_in_dim(lower_inv, new_low, low_no, 0)
        upper_inv = lax.dynamic_update_index_in_dim(upper_inv, new_up, up_no, 0)
        return (upper_inv, lower_inv)

    start = jnp.zeros((size, size), jnp.float32)
    return lax.fori_loop(0, size, row_step, (start, start))


def global_index(count_items, block_size, group_count, my_place):
    positions = jnp.arange(count_items, dtype=jnp.int32)
    return (positions // block_size * group_count + my_place) * block_size + positions % block_size


def trace_sources(pivots, first_row, count, targets):

    def back_step(step_no, sources):
        column_no = (first_row + count - 1 - step_no).astype(jnp.int32)
        partner = pivots[column_no]
        return jnp.where(
            sources == column_no, partner, jnp.where(sources == partner, column_no, sources)
        )

    return lax.fori_loop(0, count, back_step, targets)


def swap_rows(held, pivots, first_row, count, block_size, prow_count, my_prow):
    rows_local = held.shape[0]
    targets = jnp.concatenate([first_row + jnp.arange(count, dtype=jnp.int32), pivots])
    sources = trace_sources(pivots, first_row, count, targets)
    source_mine = sources // block_size % prow_count == my_prow
    source_local = sources // (block_size * prow_count) * block_size + sources % block_size
    fetched = jnp.take(held, jnp.where(source_mine, source_local, 0), axis=0)
    contrib = jnp.where(source_mine[:, None], fetched, 0.0)
    moved_rows = lax.psum(contrib, "prow")
    target_mine = targets // block_size % prow_count == my_prow
    target_local = targets // (block_size * prow_count) * block_size + targets % block_size
    held = held.at[jnp.where(target_mine, target_local, rows_local)].set(moved_rows, mode="drop")
    return (held, moved_rows)


def local(matrix, pivots):
    row_blocks = matrix.shape[0]
    block_size = matrix.shape[2]
    col_blocks = matrix.shape[3]
    prow_count = lax.axis_size("prow")
    pcol_count = lax.axis_size("pcol")
    my_prow = lax.axis_index("prow")
    my_pcol = lax.axis_index("pcol")
    rows_local = row_blocks * block_size
    cols_local = col_blocks * block_size
    held = matrix.reshape(rows_local, cols_local)
    row_global = global_index(rows_local, block_size, prow_count, my_prow)
    col_global = global_index(cols_local, block_size, pcol_count, my_pcol)
    owner_prow = 0 % prow_count
    row_slot = 0 // prow_count
    owner_pcol = 0 % pcol_count
    col_slot = 0 // pcol_count
    row_lo = row_slot * block_size
    col_lo = col_slot * block_size
    held, moved_rows = swap_rows(held, pivots, 0, block_size, block_size, prow_count, my_prow)
    panel_cols = held
    diag_raw = from_root(
        held[row_lo : row_lo + block_size, col_lo : col_lo + block_size], "prow", owner_prow
    )
    row_raw = held[row_lo : row_lo + block_size]
    below = row_global >= block_size
    packed = eliminate(diag_raw)
    upper_inv, lower_inv = both_inverses(packed)
    solved_cols = jnp.dot(
        panel_cols, upper_inv, precision=lax.Precision.HIGHEST, preferred_element_type=jnp.float32
    )
    payload = jnp.concatenate([jnp.where(below[:, None], solved_cols, 0.0), packed, lower_inv], 0)
    received = from_root(payload, "pcol", owner_pcol)
    left_op = received[:rows_local]
    packed = received[rows_local : rows_local + block_size]
    lower_inv = received[rows_local + block_size :]
    solved = jnp.dot(
        lower_inv, row_raw, precision=lax.Precision.HIGHEST, preferred_element_type=jnp.float32
    )
    row_final = from_root(solved, "prow", owner_prow)
    trailing_cols = col_global >= block_size
    right_op = jnp.where(trailing_cols[None, :], row_final, 0.0)
    held = held - jnp.dot(
        left_op, right_op, precision=lax.Precision.HIGHEST, preferred_element_type=jnp.float32
    )
    panel_new = jnp.where(below[:, None], left_op, panel_cols)
    panel_tiles = panel_new.reshape(row_blocks, block_size, block_size)
    panel_tiles = panel_tiles.at[row_slot].set(
        jnp.where(my_prow == owner_prow, packed, panel_tiles[row_slot])
    )
    held = held.at[:, col_lo : col_lo + block_size].set(
        jnp.where(my_pcol == owner_pcol, panel_tiles.reshape(rows_local, block_size), held)
    )
    keep_rows = (my_prow == owner_prow) & trailing_cols[None, :]
    held = held.at[row_lo : row_lo + block_size].set(
        jnp.where(keep_rows, row_final, held[row_lo : row_lo + block_size])
    )
    return held.reshape(matrix.shape)


def solution(mesh):
    return jax.shard_map(
        local,
        mesh=mesh,
        in_specs=(P(None, "prow", None, None, "pcol", None), P()),
        out_specs=P(None, "prow", None, None, "pcol", None),
        check_vma=False,
    )
```

profile of v0, /device:TPU:48, one launch (start us, length us, event | category | flops | bytes accessed | tf_op | source)
XLA Modules:
  0.0 876.3 jit_solution(12851266730310642802)
XLA Ops:
  6.5 7.0 copy.43
  13.6 150.0 %while.53 = (s32[]{:T(128)}, s32[256]{0:T(256)S(1)}, s32[128]{0:T(128)S(1)}, s32[]{:T(128)}, s32[]{:T(128)}, /*index=5*/s32[]{:T(128)}, s32[]{:T(128)}) while((s32[]{:T(128)}, s32[256]{0:T(256)S(1)}, s32[128]{0:T(128)S(1)}, s32[]{:T(128)}, s32[]{:T(128)}, /*index=5*/s32[]{:T(128)}, s32[]{:T(128)}) %tuple.142), condition=%wide.region_1.2_spmd, body=%wide.region_0.1_spmd.sunk | while | flops 1030 | bytes 2191 | solution.py:80
  163.6 4.1 gather_fusion
  167.7 0.8 select_select_fusion
  168.6 43.2 %all-reduce.5.cloned.1.call-done = f32[256,128]{1,0:T(8,128)} async-done(((f32[256,128]{1,0:T(8,128)}), f32[256,128]{1,0:T(8,128)}) %all-reduce.5.cloned.1.call-update) | async-done | bytes 131088 | tf_op jit(solution)/shard_map/psum | solution.py:91
  211.8 8.2 scatter_fusion
  220.1 1.5 slice_select_fusion.3
  221.7 41.6 %all-reduce.7.cloned.1.call-done = f32[128,128]{1,0:T(8,128)} async-done(((f32[128,128]{1,0:T(8,128)}), f32[128,128]{1,0:T(8,128)}) %all-reduce.7.cloned.1.call-update) | async-done | bytes 65552 | tf_op jit(solution)/shard_map/psum | solution.py:9
  263.3 0.9 copy.4
  264.2 180.8 %while.54 = (s32[]{:T(128)}, f32[128,128]{0,1:T(8,128)S(1)}, s32[]{:T(128)}) while((s32[]{:T(128)}, f32[128,128]{0,1:T(8,128)S(1)}, s32[]{:T(128)}) %tuple.128), condition=%wide.region_6.7_spmd.clone.clone, body=%wide.region_5.6_spmd.clone.clone.sunk | while | flops 66434 | bytes 268349 | solution.py:27
  445.3 197.9 %while.55 = (s32[]{:T(128)}, f32[128,128]{1,0:T(8,128)S(1)}, f32[128,128]{1,0:T(8,128)S(1)}, f32[128,128]{1,0:T(8,128)S(1)}, f32[128]{0:T(128)S(1)}, /*index=5*/...) while((s32[]{:T(128)}, f32[128,128]{1,0:T(8,128)S(1)}, ...), condition=%wide.region_9.10_spmd.clone.clone, body=%wide.region_8.9_spmd.clone.clone.sunk | while | flops 394118 | bytes 136371 | solution.py:63
  445.9 0.7 fusion.73
  447.4 0.7 fusion.73
  643.1 18.9 %convolution_select_fusion = f32[16384,128]{1,0:T(8,128)S(1)} fusion(f32[16384,128]{1,0:T(8,128)} %scatter_fusion, f32[128,128]{1,0:T(8,128)S(1)} %get-tuple-element.386, pred[16384]{0:T(1024)(128)(4,1)S(1)} %fusion.29), kind=kOutput, calls=%fused_computation.32 | convolution fusion | flops 3223322624 | bytes 16859136 | tf_op jit(solution)/shard_map/dot_general | solution.py:126
  662.1 8.7 maximum_select_fusion
  671.1 119.3 %all-reduce.9.cloned.1.call-done = f32[16640,128]{1,0:T(8,128)} async-done(((f32[16640,128]{1,0:T(8,128)}), f32[16640,128]{1,0:T(8,128)}) %all-reduce.9.cloned.1.call-update) | async-done | bytes 8519696 | tf_op jit(solution)/shard_map/psum | solution.py:9
  790.4 9.8 %slice_select_fusion = f32[16384,128]{1,0:T(8,128)S(1)} fusion(f32[16384,128]{1,0:T(8,128)} %scatter_fusion, f32[16640,128]{1,0:T(8,128)} %all-reduce.9.cloned.1.call-done, pred[16384]{0:T(1024)(128)(4,1)S(1)} %fusion.29), kind=kLoop, calls=%fused_computation.35 | loop fusion | flops 2097152 | bytes 25182208 | tf_op jit(solution)/shard_map/jit(_where)/select_n | solution.py:143
  800.2 3.3 copy.39
  803.5 2.5 copy-done
  806.0 1.7 convolution_select_fusion.1
  807.7 1.5 fusion.34
  809.2 40.7 %all-reduce.11.cloned.1.call-done = f32[128,128]{1,0:T(8,128)} async-done(((f32[128,128]{1,0:T(8,128)}), f32[128,128]{1,0:T(8,128)}) %all-reduce.11.cloned.1.call-update) | async-done | bytes 65552 | tf_op jit(solution)/shard_map/psum | solution.py:9
  849.9 16.4 %fusion.17 = f32[16384,128]{1,0:T(8,128)S(1)} fusion(f32[16384,128]{1,0:T(8,128)} %bitcast.90, f32[16384,128]{1,0:T(8,128)} %scatter_fusion, f32[16640,128]{1,0:T(8,128)} %all-reduce.9.cloned.1.call-done, pred[]{:T(512)S(6)} %eq.133, f32[128,128]{1,0:T(8,128)} %all-reduce.11.cloned.1.call-done, pred[128]{0:T(512)(128)(4,1)S(1)} %fusion.49), kind=kOutput, calls=%fused_computation.31 | convolution fusion | flops 3225436160 | bytes 33620096 | tf_op jit(solution)/shard_map/dot_general | solution.py:140
  866.4 3.4 copy-done.1
  (1690 shorter events, 514.1 us)
Async XLA Ops:
  6.5 7.0 copy-start.3
  6.5 205.3 %all-reduce.5.cloned.1.call-start = ((), (), s32[]{:S(2)}) async-start(), calls=%async_computation | async-start | bytes 262144 | tf_op jit(solution)/shard_map/psum | solution.py:91
  168.5 94.8 %all-reduce.7.cloned.1.call-start = ((), (), s32[]{:S(2)}) async-start(), calls=%async_computation.1 | async-start | bytes 131072 | tf_op jit(solution)/shard_map/psum | solution.py:9
  221.6 568.8 %all-reduce.9.cloned.1.call-start = ((), (), s32[]{:S(2)}) async-start(), calls=%async_computation.2 | async-start | bytes 17039360 | tf_op jit(solution)/shard_map/psum | solution.py:9
  670.9 179.1 %all-reduce.11.cloned.1.call-start = ((), (), s32[]{:S(2)}) async-start(), calls=%async_computation.3 | async-start | bytes 131072 | tf_op jit(solution)/shard_map/psum | solution.py:9
  800.2 5.7 copy-start
  849.9 16.4 %copy-start.2 = (f32[128,128]{1,0:T(8,128)S(1)}, f32[128,128]{1,0:T(8,128)}, u32[]{:S(2)}) copy-start(f32[128,128]{1,0:T(8,128)} %all-reduce.11.cloned.1.call-done) | copy-start | bytes 196612
  866.4 3.4 copy-start.1
Sparse Core Ops, SparseCore 0:
  168.6 43.1 all-reduce.4
  221.7 41.5 all-reduce.6
  671.0 119.3 all-reduce.8
  807.8 42.0 all-reduce.10
where the time goes:
time: 881 us; the launch traced here: 876 us
  local copies, waits for them, and re-layouts  272 us (31%)
  waiting for transfers between devices  245 us (28%)
  other arithmetic  184 us (21%)
  matrix products  148 us (17%)
  loops' own time  13.9 us (2%)
  between operations  13.3 us (2%)
    psum x3, waiting for transfers between devices, from_root(): return lax.psum(kept, axis)  202 us
    dot_general x128, matrix products, row_step(): jnp.dot(up_row, upper_inv, precision=lax.Precision.HIGHEST, preferred_ele...  90.9 us
    dynamic_slice x128, local copies, waits for them, and re-layouts, reduce_step(): pivot_value = factors[column_no, column_no]  74.4 us
    dynamic_slice x128, local copies, waits for them, and re-layouts, back_step(): partner = pivots[column_no]  74.2 us
    dynamic_slice x128, local copies, waits for them, and re-layouts, row_step(): lax.dynamic_index_in_dim(diag_values, up_no, 0, keepdims=False)  74.2 us
    broadcast_in_dim x128, other arithmetic, reduce_step(): jnp.where(below[:, None] & (positions[None, :] == column_no), multiplier[...  72.6 us
    select_n x128, other arithmetic, back_step(): jnp.where(sources == column_no, partner, jnp.where(sources == partner, co...  72.6 us
    psum x1, waiting for transfers between devices, swap_rows(): moved_rows = lax.psum(contrib, 'prow')  43.2 us
  transfers between devices with their start and end apart: 4, of which 4 were waited for; matrix products, arithmetic and copies ran while one was open for 0% of the time, Pallas kernels for 0%

commit v1 on v0

v1 whole, which is shorter than its diff:
```python
import functools

import jax
import jax.numpy as jnp
from jax import lax
from jax.experimental import pallas as pl
from jax.experimental.pallas import tpu as pltpu
from jax.sharding import PartitionSpec as P

MESH = pl.DeviceIdType.MESH
F32 = jnp.float32
BF16 = jnp.bfloat16
NB = 128
SIDE = 4
TREES = 4
STEPS = ((1, 0), (-1, 0), (0, 1), (0, -1))
SENDERS = ((0, 4, 8, 11, 5, 6, 9, 10), (7, 5, 6), (4, 5), (4, 8))
DEPTHS = (0, 3, 4, 3, 1, 2, 3, 2, 2, 3, 4, 3, 3, 4, 5, 4)
MAX_DEPTH = max(DEPTHS)
SKEW = 6
CHUNK = 128
PIECES = 4
READY = 38
VMEM_MIB = 40


def one_of(value, places):
    found = value == places[0]
    for place in places[1:]:
        found = jnp.logical_or(found, value == place)
    return found


def turn(step, times):
    for _ in range(times):
        step = (-step[1], step[0])
    return step


def eliminate_and_invert(a_ref, inv_ref):
    n, b = NB, 8
    lanes1 = lax.broadcasted_iota(jnp.int32, (1, n), 1)
    lanes8 = lax.broadcasted_iota(jnp.int32, (b, n), 1)
    subl = lax.broadcasted_iota(jnp.int32, (b, n), 0)
    rows = lax.broadcasted_iota(jnp.int32, (n, n), 0)
    lanes = lax.broadcasted_iota(jnp.int32, (n, n), 1)
    inv_ref[...] = jnp.zeros((n, n), F32)

    def block(k, carry):
        c0 = pl.multiple_of(k * b, b)

        def pick(x, j):
            return jnp.take_along_axis(x, jnp.full(x.shape, c0 + j, jnp.int32), axis=1)

        row = a_ref[pl.ds(c0, b), :]
        irow = inv_ref[pl.ds(c0, b), :]
        cols = [pick(row, j) for j in range(b)]
        recs, us, prow, pinv, gs = [], {}, [], [], []
        for s in range(b):
            r = 1.0 / jnp.broadcast_to(cols[s][s : s + 1], (b, n))
            recs.append(r[0:1])
            g = jnp.where(subl > s, cols[s] * r, 0.0)
            gs.append(g)
            for j in range(s + 1, b):
                us[s, j] = cols[j][s : s + 1]
                cols[j] = cols[j] - g * us[s, j]
            ar = jnp.where(lanes1 > c0 + s, row[s : s + 1], 0.0)
            row = row - g * ar
            ir = jnp.where(lanes1 == c0 + s, 1.0, irow[s : s + 1])
            irow = irow - g * ir
            prow.append(ar)
            pinv.append(ir)
        for s in range(b):
            row = jnp.where((lanes8 == c0 + s) & (subl > s), gs[s], row)
        whole = a_ref[...]
        inverse = inv_ref[...]
        below = rows >= c0 + b
        own = jnp.where(rows == lanes, 1.0, 0.0)
        mix = jnp.where(below, whole, jnp.where(rows < c0, inverse, own))
        mult = []
        for j in range(b):
            c = pick(mix, j)
            for s in range(j):
                c = c - mult[s] * us[s, j]
            mult.append(c * recs[j])
        upd = whole
        iupd = jnp.where((rows >= c0) & (rows < c0 + b), 0.0, inverse)
        for s in range(b):
            upd = upd - mult[s] * prow[s]
            iupd = iupd - mult[s] * jnp.where(below, pinv[s], prow[s])
        for s in range(b):
            at = lanes == c0 + s
            upd = jnp.where(at, mult[s], upd)
            iupd = jnp.where(at & jnp.logical_not(below), mult[s], iupd)
        a_ref[...] = jnp.where(below, upd, whole)
        inv_ref[...] = iupd
        a_ref[pl.ds(c0, b), :] = row
        inv_ref[pl.ds(c0, b), :] = jnp.where(lanes8 < c0 + subl, irow, inv_ref[pl.ds(c0, b), :])
        return carry

    lax.fori_loop(0, n // b, block, 0)


def exchange_kernel(
    piv_s, piv_v, mat, held, fix,
    panel, contrib, xbuf, dbuf, moved, diag, low_rows, inv, packed, right_upper, right_rows, src_v, src_s,
    load_sem, piece_sem, src_sem, recv_sem, tree_sem, part_sem, x_send, x_recv, d_send, d_recv,
    z_send, y_send, f_recv, c_send, c_recv,
):
    rows_local = held.shape[0]
    share = rows_local // TREES
    chunks = share // CHUNK
    per_piece = chunks // PIECES
    piece_rows = per_piece * CHUNK
    px = lax.axis_index("prow")
    pc = lax.axis_index("pcol")
    core = lax.rem(pc, 2)
    chip = lax.div(pc, 2)
    y = lax.div(chip, SIDE)
    z = lax.rem(chip, SIDE)
    is_root = pc == 0
    is_root1 = pc == 1
    partner = (px, pc + 1 - 2 * core)

    def pcol_of(yy, zz):
        return (lax.rem(yy + SIDE, SIDE) * SIDE + lax.rem(zz + SIDE, SIDE)) * 2 + core

    x_peers = [(lax.rem(px + k, SIDE), pc) for k in range(1, SIDE)]
    y_peers = [(px, pcol_of(y + k, z)) for k in range(1, SIDE)]
    z_peers = [(px, pcol_of(y, z + k)) for k in range(1, SIDE)]
    cross = [(lax.rem(px + k, SIDE), 1 - pc) for k in range(1, SIDE)]

    def remote(src, dst, send, recv, where):
        return pltpu.make_async_remote_copy(
            src_ref=src, dst_ref=dst, send_sem=send, recv_sem=recv, device_id=where, device_id_type=MESH
        )

    hold = pltpu.make_async_copy(mat, held, load_sem)
    pieces = []
    for q in range(PIECES):
        for t in range(TREES):
            part = pl.ds(t * share + q * piece_rows, piece_rows)
            pieces.append(pltpu.make_async_copy(mat.at[part], panel.at[part], piece_sem.at[q * TREES + t]))

    @pl.when(is_root)
    def _():
        for piece in pieces:
            piece.start()

    @pl.when(jnp.logical_not(is_root))
    def _():
        hold.start()

    barrier = pltpu.get_barrier_semaphore()
    for where in x_peers + y_peers + z_peers + [partner]:
        pl.semaphore_signal(barrier, inc=1, device_id=where, device_id_type=MESH)

    @pl.when(pc < 2)
    def _():
        for where in cross:
            pl.semaphore_signal(barrier, inc=1, device_id=where, device_id_type=MESH)

    which = lax.broadcasted_iota(jnp.int32, (8, NB), 0)
    sources = jnp.where(which == 0, lax.broadcasted_iota(jnp.int32, (8, NB), 1), piv_v[...])

    def back(step, sources):
        column = NB - 1 - step
        other = piv_s[column]
        return jnp.where(sources == column, other, jnp.where(sources == other, column, sources))

    src_v[...] = lax.fori_loop(0, NB, back, sources)
    to_scalars = pltpu.make_async_copy(src_v, src_s, src_sem)
    to_scalars.start()

    @pl.when(pc < 2)
    def _():
        pl.semaphore_wait(barrier, 13)

    @pl.when(pc >= 2)
    def _():
        pl.semaphore_wait(barrier, 10)

    feeds, depth, targets = [], [], []
    for t in range(TREES):
        yy, zz = y, z
        for _ in range(t):
            yy, zz = zz, lax.rem(SIDE - yy, SIDE)
        place = yy * SIDE + zz
        feeds.append([one_of(place, SENDERS[d]) for d in range(4)])
        level = 0
        for where in range(1, SIDE * SIDE):
            level = level + jnp.where(place == where, DEPTHS[where], 0)
        depth.append(level)
        targets.append([])
        for d in range(4):
            dy, dz = turn(STEPS[d], t)
            targets[t].append((px, pcol_of(y + dy, z + dz)))

    def chunk_at(t, c):
        return panel.at[pl.ds(pl.multiple_of(t * share + c * CHUNK, CHUNK), CHUNK)]

    def forward(t, c):
        block = chunk_at(t, c)
        arrival = recv_sem.at[t * chunks + c]
        for d in range(4):

            @pl.when(feeds[t][d])
            def _():
                remote(block, block, tree_sem.at[t * 4 + d], arrival, targets[t][d]).start()

        remote(block, block, part_sem.at[t], arrival, partner).start()

    def forward_range(lo, hi):
        def one(c, carry):
            for t in range(TREES):
                forward(t, c)
            return carry

        lax.fori_loop(lo, hi, one, 0)

    to_scalars.wait()

    def gather_from(rows_ref):
        def gather(g, carry):
            for r in range(2):
                base = pl.multiple_of(g * 8, 8)
                found = []
                for s in range(8):
                    source = src_s[r, g * 8 + s]
                    block = lax.div(source, NB)
                    mine = lax.rem(block, SIDE) == px
                    local = lax.div(block, SIDE) * NB + lax.rem(source, NB)
                    row = rows_ref[pl.ds(jnp.where(mine, local, 0), 1), :]
                    found.append(jnp.where(mine, row, 0.0))
                contrib[pl.ds(r * NB + base, 8), :] = jnp.concatenate(found, axis=0)
            return carry

        lax.fori_loop(0, NB // 8, gather, 0)

    @pl.when(is_root)
    def _():
        for piece in pieces[:TREES]:
            piece.wait()
        forward_range(0, per_piece)
        for piece in pieces[TREES:]:
            piece.wait()
        gather_from(panel)

    @pl.when(jnp.logical_not(is_root))
    def _():
        hold.wait()
        gather_from(held)

    d_copies = []
    for k in range(SIDE):
        where = (lax.rem(px + k, SIDE), pc + 1)
        d_copies.append(remote(contrib, dbuf.at[px], d_send.at[k], d_recv.at[px], where))

    @pl.when(is_root)
    def _():
        for copy in d_copies:
            copy.start()

    x_copies = [
        remote(contrib, xbuf.at[px], x_send.at[k], x_recv.at[px], x_peers[k]) for k in range(SIDE - 1)
    ]
    for copy in x_copies:
        copy.start()

    def arrived(ref, sem):
        pltpu.make_async_copy(ref, ref, sem).wait()

    def receive_moved():
        total = contrib[...]
        for k in range(1, SIDE):
            slot = lax.rem(px + k, SIDE)
            arrived(xbuf.at[slot], x_recv.at[slot])
            total = total + xbuf[slot]
        moved[...] = total

    def take_factors():
        receive_moved()
        upper, urows = factors(inv[...], moved[pl.ds(0, NB), :])
        right_upper[...] = right_side(upper)
        right_rows[...] = right_side(urows)

    def update(starts, size):
        places = [pl.ds(pl.multiple_of(start, CHUNK), size) for start in starts]
        old = [held[place, :] for place in places]
        upper, rows = right_upper[...], right_rows[...]
        lows = [product(panel[place, :], upper) for place in places]
        for place, x, low in zip(places, old, lows):
            held[place, :] = jnp.where(is_root, low, x - product(low, rows))

    def update_group(g, width):
        update([t * share + g * CHUNK for t in range(TREES)], width * CHUNK)

    def update_pairs(lo, hi):
        def one(m, carry):
            update_group(m * 2, 2)
            return carry

        lax.fori_loop(lo // 2, hi // 2, one, 0)

    @pl.when(is_root)
    def _():
        forward_range(per_piece, chunks)
        arrived(packed, c_recv.at[1])
        arrived(inv, c_recv.at[2])
        take_factors()
        update_pairs(0, chunks)

    steps = chunks + SKEW * MAX_DEPTH
    ready = min(READY, steps)
    done = min(steps - ready, chunks)
    done -= done % 2

    @pl.when(jnp.logical_and(core == 0, jnp.logical_not(is_root)))
    def _():
        def relay(i, carry):
            for t in range(TREES):
                c = i - SKEW * depth[t]

                @pl.when(jnp.logical_and(c >= 0, c < chunks))
                def _():
                    arrived(chunk_at(t, c), recv_sem.at[t * chunks + c])
                    forward(t, c)

            return carry

        def relay_and_update(i, carry):
            relay(i, carry)
            update_group(i - ready, 1)
            return carry

        lax.fori_loop(0, ready, relay, 0)
        arrived(packed, c_recv.at[1])
        arrived(inv, c_recv.at[2])
        take_factors()
        lax.fori_loop(ready, ready + done, relay_and_update, 0)
        lax.fori_loop(ready + done, steps, relay, 0)
        update_pairs(done, chunks)

    z_copies = [remote(diag, diag, z_send.at[k], f_recv.at[0], z_peers[k]) for k in range(3)]
    z_copies += [remote(low_rows, low_rows, z_send.at[3 + k], f_recv.at[1], z_peers[k]) for k in range(3)]
    y_copies = [remote(diag, diag, y_send.at[k], f_recv.at[0], y_peers[k]) for k in range(3)]
    y_copies += [remote(low_rows, low_rows, y_send.at[3 + k], f_recv.at[1], y_peers[k]) for k in range(3)]
    c_copies = [
        remote(low_rows, low_rows, c_send.at[0], c_recv.at[0], partner),
        remote(packed, packed, c_send.at[1], c_recv.at[1], partner),
        remote(inv, inv, c_send.at[2], c_recv.at[2], partner),
    ]

    @pl.when(core == 1)
    def _():
        @pl.when(is_root1)
        def _():
            for k in range(SIDE):
                arrived(dbuf.at[k], d_recv.at[k])
            total = dbuf[0] + dbuf[1] + dbuf[2] + dbuf[3]
            diag[...] = total[:NB]
            low_rows[...] = total[NB:]
            for k in range(3):
                z_copies[k].start()
            for k in range(3):
                y_copies[k].start()
            for k in range(3):
                z_copies[3 + k].start()
            for k in range(3):
                y_copies[3 + k].start()

        @pl.when(jnp.logical_not(is_root1))
        def _():
            arrived(diag, f_recv.at[0])

            @pl.when(y == 0)
            def _():
                for k in range(3):
                    y_copies[k].start()
                arrived(low_rows, f_recv.at[1])
                for k in range(3):
                    y_copies[3 + k].start()

        packed[...] = diag[...]
        eliminate_and_invert(packed, inv)
        c_copies[1].start()
        c_copies[2].start()

        @pl.when(y != 0)
        def _():
            arrived(low_rows, f_recv.at[1])

        c_copies[0].start()
        take_factors()

        def receive(m, carry):
            for i in (2 * m, 2 * m + 1):
                for t in range(TREES):
                    arrived(chunk_at(t, i), recv_sem.at[t * chunks + i])
            update_group(2 * m, 2)
            return carry

        lax.fori_loop(0, chunks // 2, receive, 0)

        for copy in c_copies:
            copy.wait_send()

        @pl.when(is_root1)
        def _():
            for copy in z_copies:
                copy.wait_send()

        @pl.when(y == 0)
        def _():
            for copy in y_copies:
                copy.wait_send()

    @pl.when(core == 0)
    def _():
        arrived(low_rows, c_recv.at[0])
        for t in range(TREES):
            sent = panel.at[pl.ds(t * share, share)]
            for d in range(4):

                @pl.when(feeds[t][d])
                def _():
                    remote(sent, sent, tree_sem.at[t * 4 + d], recv_sem.at[0], partner).wait_send()

            remote(sent, sent, part_sem.at[t], recv_sem.at[0], partner).wait_send()

        @pl.when(is_root)
        def _():
            for copy in d_copies:
                copy.wait_send()

    low = product(low_rows[...], right_upper[...])
    fix[...] = jnp.where(is_root, low, moved[pl.ds(NB, NB), :] - product(low, right_rows[...]))

    @pl.when(px == 0)
    def _():
        lower = moved[pl.ds(0, NB), :]
        urows = factors(inv[...], lower)[1]
        held[pl.ds(0, NB), :] = jnp.where(is_root, packed[...], urows)

    for copy in x_copies:
        copy.wait_send()


def split(x):
    high = x.astype(BF16)
    return high, (x - high.astype(F32)).astype(BF16)


def right_side(x):
    high, low = split(x)
    return jnp.concatenate(
        [jnp.concatenate([high, low], axis=1), jnp.concatenate([high, jnp.zeros_like(low)], axis=1)], axis=0
    )


def product(x, right):
    high, low = split(x)
    both = jnp.dot(jnp.concatenate([high, low], axis=1), right, preferred_element_type=F32)
    return both[:, :NB] + both[:, NB:]


def factors(inv, moved_top):
    rows = lax.broadcasted_iota(jnp.int32, (NB, NB), 0)
    lanes = lax.broadcasted_iota(jnp.int32, (NB, NB), 1)
    upper = jnp.where(rows <= lanes, inv, 0.0)
    lower = jnp.where(rows > lanes, inv, jnp.where(rows == lanes, 1.0, 0.0))
    urows = jnp.dot(lower, moved_top, precision=lax.Precision.HIGHEST, preferred_element_type=F32)
    return upper, urows


def finish_kernel(piv_s, held, fix, out, store_sem, row_sem):
    blocks = store_sem.shape[0]
    size = held.shape[0] // blocks
    px = lax.axis_index("prow")
    stores = []
    for b in range(blocks):
        part = pl.ds(b * size, size)
        stores.append(pltpu.make_async_copy(held.at[part], out.at[part], store_sem.at[b]))
    for store in stores:
        store.start()
    for store in stores:
        store.wait()

    def row_copy(j):
        target = piv_s[j]
        place = lax.div(target, NB)
        mine = jnp.logical_and(lax.rem(place, SIDE) == px, place > 0)
        local = lax.div(place, SIDE) * NB + lax.rem(target, NB)
        return mine, pltpu.make_async_copy(fix.at[pl.ds(j, 1)], out.at[pl.ds(local, 1)], row_sem)

    def start(j, carry):
        mine, copy = row_copy(j)

        @pl.when(mine)
        def _():
            copy.start()

        return carry

    def finish(j, carry):
        mine, copy = row_copy(j)

        @pl.when(mine)
        def _():
            copy.wait()

        return carry

    lax.fori_loop(0, NB, start, 0)
    lax.fori_loop(0, NB, finish, 0)


def local(matrix, pivots):
    rows_local = matrix.shape[0] * matrix.shape[2]
    held = matrix.reshape(rows_local, NB)
    chunks = rows_local // CHUNK
    smem = pl.BlockSpec(memory_space=pltpu.SMEM)
    vmem = pl.BlockSpec(memory_space=pltpu.VMEM)
    hbm = pl.BlockSpec(memory_space=pl.ANY)
    square = pltpu.VMEM((NB, NB), F32)
    dma = pltpu.SemaphoreType.DMA
    changed, fix = pl.pallas_call(
        exchange_kernel,
        out_shape=(
            jax.ShapeDtypeStruct((rows_local, NB), F32),
            jax.ShapeDtypeStruct((NB, NB), F32),
        ),
        in_specs=[smem, vmem, hbm],
        out_specs=(vmem,) * 2,
        scratch_shapes=[
            pltpu.VMEM((rows_local, NB), F32),
            pltpu.VMEM((2 * NB, NB), F32),
            pltpu.VMEM((SIDE, 2 * NB, NB), F32),
            pltpu.VMEM((SIDE, 2 * NB, NB), F32),
            pltpu.VMEM((2 * NB, NB), F32),
            square,
            square,
            square,
            square,
            pltpu.VMEM((2 * NB, 2 * NB), BF16),
            pltpu.VMEM((2 * NB, 2 * NB), BF16),
            pltpu.VMEM((8, NB), jnp.int32),
            pltpu.SMEM((8, NB), jnp.int32),
            dma,
            dma((PIECES * TREES,)),
            dma,
            dma((chunks,)),
            dma((TREES * 4,)),
            dma((TREES,)),
            dma((SIDE - 1,)),
            dma((SIDE,)),
            dma((SIDE,)),
            dma((SIDE,)),
            dma((6,)),
            dma((6,)),
            dma((2,)),
            dma((3,)),
            dma((3,)),
        ],
        compiler_params=pltpu.CompilerParams(
            collective_id=0, has_side_effects=True, vmem_limit_bytes=VMEM_MIB * 2**20
        ),
    )(pivots, pivots.reshape(1, NB), held)
    out = pl.pallas_call(
        finish_kernel,
        out_shape=jax.ShapeDtypeStruct((rows_local, NB), F32),
        in_specs=[smem, vmem, vmem],
        out_specs=hbm,
        scratch_shapes=[dma((4,)), dma],
        compiler_params=pltpu.CompilerParams(vmem_limit_bytes=4 * 2**20),
    )(pivots, changed, fix)
    return out.reshape(matrix.shape)


def solution(mesh):
    return jax.shard_map(
        local,
        mesh=mesh,
        in_specs=(P(None, "prow", None, None, "pcol", None), P()),
        out_specs=P(None, "prow", None, None, "pcol", None),
        check_vma=False,
    )
```

time: 881 us -> 59.3 us (0.07)
  local copies, waits for them, and re-layouts: 272 us -> 0.65 us
  waiting for transfers between devices: 245 us -> 0 us
  other arithmetic: 184 us -> 0 us
  matrix products: 148 us -> 0 us
  Pallas kernels: 0 us -> 58.3 us
  loops' own time: 13.9 us -> 0 us
  between operations: 13.3 us -> 0.01 us
    psum x4 -> x0, waiting for transfers between devices: 245 us -> none  [the longest x3 202 us: from_root(): return lax.psum(kept, axis)]
    dynamic_slice x384 -> x0, local copies, waits for them, and re-layouts: 223 us -> none  [the longest x128 74.4 us: reduce_step(): pivot_value = factors[column_no, column_no]]
    dot_general x259 -> x0, matrix products: 148 us -> none  [the longest x128 90.9 us: row_step(): jnp.dot(up_row, upper_inv, precision=lax.Precision.HIGHEST, preferred_ele...]
    select_n x262 -> x0, other arithmetic: 107 us -> none  [the longest x128 72.6 us: back_step(): jnp.where(sources == column_no, partner, jnp.where(sources == partner, co...]
    broadcast_in_dim x128 -> x0, other arithmetic: 72.6 us -> none  [reduce_step(): jnp.where(below[:, None] & (positions[None, :] == column_no), multiplier[...]
    pallas_call x0 -> x2, Pallas kernels: none -> 58.3 us  [the longest x1 51.7 us: local(): pl.pallas_call(exchange_kernel, out_shape=(jax.ShapeDtypeStruct((rows_loc...]
    unnamed x11 -> x2, local copies, waits for them, and re-layouts: 17.1 us -> 0.65 us
    another operation x3 -> x0, loops' own time: 13.9 us -> none  [the longest x1 6.53 us: eliminate(): return lax.fori_loop(0, size, reduce_step, square)]
  transfers between devices with their start and end apart: 4 -> 0, of which waited for: 4 -> 0; matrix products, arithmetic and copies ran while one was open for 0% -> 0% of each run, Pallas kernels for 0% -> 0%
where the time goes in v1:
time: 59.3 us; the launch traced here: 59 us
  Pallas kernels  58.3 us (98%)
  local copies, waits for them, and re-layouts  0.65 us (1%)
    pallas_call x1, Pallas kernels, local(): pl.pallas_call(exchange_kernel, out_shape=(jax.ShapeDtypeStruct((rows_loc...  51.7 us
    pallas_call x1, Pallas kernels, local(): pl.pallas_call(finish_kernel, out_shape=jax.ShapeDtypeStruct((rows_local,...  6.67 us

profile of v1, /device:TPU:48, one launch (start us, length us, event | category | flops | bytes accessed | tf_op | source)
XLA Modules:
  0.0 59.0 jit_solution(16380895632303281969)
XLA Ops:
  0.0 0.0 copy-start
  0.0 0.7 %copy-done = s32[128]{0:T(128)S(1)} copy-done((s32[128]{0:T(128)S(1)}, s32[128]{0:T(128)}, u32[]{:S(2)}) %copy-start) | copy-done | bytes 536
  0.7 51.7 %shard_map.28 = (f32[16384,128]{1,0:T(8,128)S(1)}, f32[128,128]{1,0:T(8,128)S(1)}) custom-call(s32[128]{0:T(128)S(1)} %copy-done, s32[1,128]{1,0:T(1,128)S(1)} %bitcast.5, f32[16384,128]{1,0:T(8,128)} %bitcast.6), custom_call_target="tpu_custom_call" | custom-call | tf_op jit(solution)/shard_map/pallas_call | solution.py:527
  52.3 6.7 %shard_map.29 = f32[16384,128]{1,0:T(8,128)} custom-call(s32[128]{0:T(128)S(1)} %copy-done, f32[16384,128]{1,0:T(8,128)S(1)} %get-tuple-element.7.held, f32[128,128]{1,0:T(8,128)S(1)} %get-tuple-element.8.fix), custom_call_target="tpu_custom_call" | custom-call | tf_op jit(solution)/shard_map/pallas_call | solution.py:569
Async XLA Ops:
  0.0 0.7 %copy-start = (s32[128]{0:T(128)S(1)}, s32[128]{0:T(128)}, u32[]{:S(2)}) copy-start(s32[128]{0:T(128)} %piv_s.3) | copy-start | bytes 1540

commit v2 on v1

--- a/solution.py
+++ b/solution.py
@@ -14,27 +14,38 @@
 SIDE = 4
 TREES = 4
 STEPS = ((1, 0), (-1, 0), (0, 1), (0, -1))
-SENDERS = ((0, 4, 8, 11, 5, 6, 9, 10), (7, 5, 6), (4, 5), (4, 8))
-DEPTHS = (0, 3, 4, 3, 1, 2, 3, 2, 2, 3, 4, 3, 3, 4, 5, 4)
-MAX_DEPTH = max(DEPTHS)
-SKEW = 6
+SENDERS = (
+    ((0, 4, 8, 9, 10, 11), (5, 6, 7), (4, 5, 8, 9), (4, 8)),
+    ((13, 14, 15), (0, 8, 9, 10, 11, 12, 13, 14, 15), (12, 13), (12,)),
+    ((1, 2, 5, 6), (1, 2), (0, 1, 2, 6, 10, 14), (5, 9, 13)),
+    ((3, 7), (3,), (7, 11, 15), (0, 2, 3, 6, 7, 10, 11, 14, 15)),
+)
+PLAIN, ROUND = 5, 6
 CHUNK = 128
 PIECES = 4
-READY = 38
+EARLY = 24
+READY = 36
+WIDE = 4
 VMEM_MIB = 40
 
 
 def one_of(value, places):
-    found = value == places[0]
-    for place in places[1:]:
+    found = value < 0
+    for place in places:
         found = jnp.logical_or(found, value == place)
     return found
 
 
-def turn(step, times):
-    for _ in range(times):
-        step = (-step[1], step[0])
-    return step
+def lags(tree):
+    lag = {0: 0}
+    while len(lag) < SIDE * SIDE:
+        for d, places in enumerate(SENDERS[tree]):
+            for place in places:
+                if place in lag:
+                    y, z = place // SIDE + STEPS[d][0], place % SIDE + STEPS[d][1]
+                    plain = 0 <= y < SIDE and 0 <= z < SIDE
+                    lag[y % SIDE * SIDE + z % SIDE] = lag[place] + (PLAIN if plain else ROUND)
+    return [lag[place] for place in range(SIDE * SIDE)]
 
 
 def eliminate_and_invert(a_ref, inv_ref):
@@ -102,9 +113,9 @@
 
 
 def exchange_kernel(
-    piv_s, piv_v, mat, held, fix,
-    panel, contrib, xbuf, dbuf, moved, diag, low_rows, inv, packed, right_upper, right_rows, src_v, src_s,
-    load_sem, piece_sem, src_sem, recv_sem, tree_sem, part_sem, x_send, x_recv, d_send, d_recv,
+    pivots, mat, held, fix,
+    panel, contrib, xbuf, dbuf, moved, diag, low_rows, inv, packed, right_upper, right_rows, src_v, src_s, piv_v, piv_s,
+    pivot_sem, load_sem, piece_sem, src_sem, recv_sem, tree_sem, part_sem, x_send, x_recv, d_send, d_recv,
     z_send, y_send, f_recv, c_send, c_recv,
 ):
     rows_local = held.shape[0]
@@ -135,6 +146,13 @@
             src_ref=src, dst_ref=dst, send_sem=send, recv_sem=recv, device_id=where, device_id_type=MESH
         )
 
+    pivot_copies = [
+        pltpu.make_async_copy(pivots, piv_s, pivot_sem.at[0]),
+        pltpu.make_async_copy(pivots, piv_v, pivot_sem.at[1]),
+    ]
+    for copy in pivot_copies:
+        copy.start()
+
     hold = pltpu.make_async_copy(mat, held, load_sem)
     pieces = []
     for q in range(PIECES):
@@ -160,12 +178,14 @@
         for where in cross:
             pl.semaphore_signal(barrier, inc=1, device_id=where, device_id_type=MESH)
 
+    for copy in pivot_copies:
+        copy.wait()
     which = lax.broadcasted_iota(jnp.int32, (8, NB), 0)
     sources = jnp.where(which == 0, lax.broadcasted_iota(jnp.int32, (8, NB), 1), piv_v[...])
 
     def back(step, sources):
         column = NB - 1 - step
-        other = piv_s[column]
+        other = piv_s[0, column]
         return jnp.where(sources == column, other, jnp.where(sources == other, column, sources))
 
     src_v[...] = lax.fori_loop(0, NB, back, sources)
@@ -180,21 +200,14 @@
     def _():
         pl.semaphore_wait(barrier, 10)
 
-    feeds, depth, targets = [], [], []
+    feeds, delay = [], []
+    targets = [(px, pcol_of(y + dy, z + dz)) for dy, dz in STEPS]
     for t in range(TREES):
-        yy, zz = y, z
-        for _ in range(t):
-            yy, zz = zz, lax.rem(SIDE - yy, SIDE)
-        place = yy * SIDE + zz
-        feeds.append([one_of(place, SENDERS[d]) for d in range(4)])
-        level = 0
-        for where in range(1, SIDE * SIDE):
-            level = level + jnp.where(place == where, DEPTHS[where], 0)
-        depth.append(level)
-        targets.append([])
-        for d in range(4):
-            dy, dz = turn(STEPS[d], t)
-            targets[t].append((px, pcol_of(y + dy, z + dz)))
+        feeds.append([one_of(chip, SENDERS[t][d]) for d in range(4)])
+        late = 0
+        for place, lag in enumerate(lags(t)):
+            late = late + jnp.where(chip == place, lag, 0)
+        delay.append(late)
 
     def chunk_at(t, c):
         return panel.at[pl.ds(pl.multiple_of(t * share + c * CHUNK, CHUNK), CHUNK)]
@@ -206,7 +219,7 @@
 
             @pl.when(feeds[t][d])
             def _():
-                remote(block, block, tree_sem.at[t * 4 + d], arrival, targets[t][d]).start()
+                remote(block, block, tree_sem.at[t * 4 + d], arrival, targets[d]).start()
 
         remote(block, block, part_sem.at[t], arrival, partner).start()
 
@@ -279,7 +292,6 @@
         moved[...] = total
 
     def take_factors():
-        receive_moved()
         upper, urows = factors(inv[...], moved[pl.ds(0, NB), :])
         right_upper[...] = right_side(upper)
         right_rows[...] = right_side(urows)
@@ -295,31 +307,33 @@
     def update_group(g, width):
         update([t * share + g * CHUNK for t in range(TREES)], width * CHUNK)
 
-    def update_pairs(lo, hi):
+    def update_rest(lo, hi):
         def one(m, carry):
-            update_group(m * 2, 2)
+            update_group(m * WIDE, WIDE)
             return carry
 
-        lax.fori_loop(lo // 2, hi // 2, one, 0)
+        lax.fori_loop(lo // WIDE, hi // WIDE, one, 0)
 
     @pl.when(is_root)
     def _():
         forward_range(per_piece, chunks)
+        receive_moved()
         arrived(packed, c_recv.at[1])
         arrived(inv, c_recv.at[2])
         take_factors()
-        update_pairs(0, chunks)
-
-    steps = chunks + SKEW * MAX_DEPTH
+        update_rest(0, chunks)
+
+    steps = chunks + max(max(lags(t)) for t in range(TREES))
     ready = min(READY, steps)
     done = min(steps - ready, chunks)
-    done -= done % 2
+    ready += done % WIDE
+    done -= done % WIDE
 
     @pl.when(jnp.logical_and(core == 0, jnp.logical_not(is_root)))
     def _():
         def relay(i, carry):
             for t in range(TREES):
-                c = i - SKEW * depth[t]
+                c = i - delay[t]
 
                 @pl.when(jnp.logical_and(c >= 0, c < chunks))
                 def _():
@@ -333,13 +347,16 @@
             update_group(i - ready, 1)
             return carry
 
-        lax.fori_loop(0, ready, relay, 0)
+        early = min(EARLY, ready)
+        lax.fori_loop(0, early, relay, 0)
+        receive_moved()
+        lax.fori_loop(early, ready, relay, 0)
         arrived(packed, c_recv.at[1])
         arrived(inv, c_recv.at[2])
         take_factors()
         lax.fori_loop(ready, ready + done, relay_and_update, 0)
         lax.fori_loop(ready + done, steps, relay, 0)
-        update_pairs(done, chunks)
+        update_rest(done, chunks)
 
     z_copies = [remote(diag, diag, z_send.at[k], f_recv.at[0], z_peers[k]) for k in range(3)]
     z_copies += [remote(low_rows, low_rows, z_send.at[3 + k], f_recv.at[1], z_peers[k]) for k in range(3)]
@@ -391,6 +408,7 @@
             arrived(low_rows, f_recv.at[1])
 
         c_copies[0].start()
+        receive_moved()
         take_factors()
 
         def receive(m, carry):
@@ -473,7 +491,7 @@
     return upper, urows
 
 
-def finish_kernel(piv_s, held, fix, out, store_sem, row_sem):
+def finish_kernel(piv_s, held, fix, out, rows_s, store_sem, row_sem):
     blocks = store_sem.shape[0]
     size = held.shape[0] // blocks
     px = lax.axis_index("prow")
@@ -483,36 +501,33 @@
         stores.append(pltpu.make_async_copy(held.at[part], out.at[part], store_sem.at[b]))
     for store in stores:
         store.start()
-    for store in stores:
-        store.wait()
-
-    def row_copy(j):
+
+    def note(j, count):
         target = piv_s[j]
         place = lax.div(target, NB)
         mine = jnp.logical_and(lax.rem(place, SIDE) == px, place > 0)
-        local = lax.div(place, SIDE) * NB + lax.rem(target, NB)
-        return mine, pltpu.make_async_copy(fix.at[pl.ds(j, 1)], out.at[pl.ds(local, 1)], row_sem)
-
-    def start(j, carry):
-        mine, copy = row_copy(j)
-
-        @pl.when(mine)
-        def _():
-            copy.start()
-
+        rows_s[0, count] = lax.div(place, SIDE) * NB + lax.rem(target, NB)
+        rows_s[1, count] = j
+        return count + jnp.where(mine, 1, 0)
+
+    count = lax.fori_loop(0, NB, note, jnp.int32(0), unroll=8)
+    for store in stores:
+        store.wait()
+
+    def row_copy(i):
+        here, there = rows_s[1, i], rows_s[0, i]
+        return pltpu.make_async_copy(fix.at[pl.ds(here, 1)], out.at[pl.ds(there, 1)], row_sem)
+
+    def start(i, carry):
+        row_copy(i).start()
         return carry
 
-    def finish(j, carry):
-        mine, copy = row_copy(j)
-
-        @pl.when(mine)
-        def _():
-            copy.wait()
-
+    def finish(i, carry):
+        row_copy(0).wait()
         return carry
 
-    lax.fori_loop(0, NB, start, 0)
-    lax.fori_loop(0, NB, finish, 0)
+    lax.fori_loop(0, count, start, 0)
+    lax.fori_loop(0, count, finish, 0)
 
 
 def local(matrix, pivots):
@@ -530,7 +545,7 @@
             jax.ShapeDtypeStruct((rows_local, NB), F32),
             jax.ShapeDtypeStruct((NB, NB), F32),
         ),
-        in_specs=[smem, vmem, hbm],
+        in_specs=[pl.BlockSpec(memory_space=pltpu.HBM), hbm],
         out_specs=(vmem,) * 2,
         scratch_shapes=[
             pltpu.VMEM((rows_local, NB), F32),
@@ -546,6 +561,9 @@
             pltpu.VMEM((2 * NB, 2 * NB), BF16),
             pltpu.VMEM((8, NB), jnp.int32),
             pltpu.SMEM((8, NB), jnp.int32),
+            pltpu.VMEM((1, NB), jnp.int32),
+            pltpu.SMEM((1, NB), jnp.int32),
+            dma((2,)),
             dma,
             dma((PIECES * TREES,)),
             dma,
@@ -565,13 +583,13 @@
         compiler_params=pltpu.CompilerParams(
             collective_id=0, has_side_effects=True, vmem_limit_bytes=VMEM_MIB * 2**20
         ),
-    )(pivots, pivots.reshape(1, NB), held)
+    )(pltpu.with_memory_space_constraint(pivots.reshape(1, NB), pltpu.HBM), held)
     out = pl.pallas_call(
         finish_kernel,
         out_shape=jax.ShapeDtypeStruct((rows_local, NB), F32),
         in_specs=[smem, vmem, vmem],
         out_specs=hbm,
-        scratch_shapes=[dma((4,)), dma],
+        scratch_shapes=[pltpu.SMEM((2, 2 * NB), jnp.int32), dma((4,)), dma],
         compiler_params=pltpu.CompilerParams(vmem_limit_bytes=4 * 2**20),
     )(pivots, changed, fix)
     return out.reshape(matrix.shape)

time: 59.3 us -> 54.7 us (0.922)
  Pallas kernels: 58.3 us -> 54.2 us
  local copies, waits for them, and re-layouts: 0.65 us -> 0.01 us
    pallas_call x1, Pallas kernels: 6.67 us -> 4.56 us  [local(): pl.pallas_call(finish_kernel, out_shape=jax.ShapeDtypeStruct((rows_local,...]
    pallas_call x1, Pallas kernels: 51.7 us -> 49.7 us  [local(): pl.pallas_call(exchange_kernel, out_shape=(jax.ShapeDtypeStruct((rows_loc...]
    unnamed x2, local copies, waits for them, and re-layouts: 0.65 us -> 0.01 us
where the time goes in v2:
time: 54.7 us; the launch traced here: 54.3 us
  Pallas kernels  54.2 us (99%)
    pallas_call x1, Pallas kernels, local(): pl.pallas_call(exchange_kernel, out_shape=(jax.ShapeDtypeStruct((rows_loc...  49.7 us
    pallas_call x1, Pallas kernels, local(): pl.pallas_call(finish_kernel, out_shape=jax.ShapeDtypeStruct((rows_local,...  4.56 us

profile of v2, /device:TPU:48, one launch (start us, length us, event | category | flops | bytes accessed | tf_op | source)
XLA Modules:
  0.0 54.3 jit_solution(4618776447528502988)
XLA Ops:
  0.0 0.0 copy-start
  0.0 49.7 %shard_map.28 = (f32[16384,128]{1,0:T(8,128)S(1)}, f32[128,128]{1,0:T(8,128)S(1)}) custom-call(s32[1,128]{1,0:T(1,128)} %bitcast.5, f32[16384,128]{1,0:T(8,128)} %bitcast.6), custom_call_target="tpu_custom_call" | custom-call | tf_op jit(solution)/shard_map/pallas_call | solution.py:542
  49.7 0.0 copy-done
  49.7 4.6 %shard_map.29 = f32[16384,128]{1,0:T(8,128)} custom-call(s32[128]{0:T(128)S(1)} %copy-done, f32[16384,128]{1,0:T(8,128)S(1)} %get-tuple-element.7.held, f32[128,128]{1,0:T(8,128)S(1)} %get-tuple-element.8.fix), custom_call_target="tpu_custom_call" | custom-call | tf_op jit(solution)/shard_map/pallas_call | solution.py:587
Async XLA Ops:
  0.0 49.7 %copy-start = (s32[128]{0:T(128)S(1)}, s32[128]{0:T(128)}, u32[]{:S(2)}) copy-start(s32[128]{0:T(128)} %piv_s.1) | copy-start | bytes 1540

commit v3 on v2

--- a/solution.py
+++ b/solution.py
@@ -24,7 +24,9 @@
 CHUNK = 128
 PIECES = 4
 EARLY = 24
-READY = 36
+LOW_AT = 16
+READY = 39
+FASTER = 47
 WIDE = 4
 VMEM_MIB = 40
 
@@ -114,9 +116,9 @@
 
 def exchange_kernel(
     pivots, mat, held, fix,
-    panel, contrib, xbuf, dbuf, moved, diag, low_rows, inv, packed, right_upper, right_rows, src_v, src_s, piv_v, piv_s,
+    panel, contrib, xbuf, dbuf, moved, diag, low_rows, inv, packed, solved, right_upper, right_rows, src_v, src_s, piv_v, piv_s,
     pivot_sem, load_sem, piece_sem, src_sem, recv_sem, tree_sem, part_sem, x_send, x_recv, d_send, d_recv,
-    z_send, y_send, f_recv, c_send, c_recv,
+    z_send, y_send, f_recv, c_send, c_recv, low_tree, low_part, low_recv,
 ):
     rows_local = held.shape[0]
     share = rows_local // TREES
@@ -178,19 +180,25 @@
         for where in cross:
             pl.semaphore_signal(barrier, inc=1, device_id=where, device_id_type=MESH)
 
-    for copy in pivot_copies:
-        copy.wait()
-    which = lax.broadcasted_iota(jnp.int32, (8, NB), 0)
-    sources = jnp.where(which == 0, lax.broadcasted_iota(jnp.int32, (8, NB), 1), piv_v[...])
-
-    def back(step, sources):
-        column = NB - 1 - step
-        other = piv_s[0, column]
-        return jnp.where(sources == column, other, jnp.where(sources == other, column, sources))
-
-    src_v[...] = lax.fori_loop(0, NB, back, sources)
     to_scalars = pltpu.make_async_copy(src_v, src_s, src_sem)
-    to_scalars.start()
+
+    def find_sources():
+        for copy in pivot_copies:
+            copy.wait()
+        which = lax.broadcasted_iota(jnp.int32, (8, NB), 0)
+        sources = jnp.where(which == 0, lax.broadcasted_iota(jnp.int32, (8, NB), 1), piv_v[...])
+
+        def back(step, sources):
+            column = NB - 1 - step
+            other = piv_s[0, column]
+            return jnp.where(sources == column, other, jnp.where(sources == other, column, sources))
+
+        src_v[...] = lax.fori_loop(0, NB, back, sources, unroll=8)
+        to_scalars.start()
+
+    @pl.when(jnp.logical_not(is_root))
+    def _():
+        find_sources()
 
     @pl.when(pc < 2)
     def _():
@@ -223,6 +231,19 @@
 
         remote(block, block, part_sem.at[t], arrival, partner).start()
 
+    def low_piece(t):
+        return low_rows.at[pl.ds(t * (NB // TREES), NB // TREES)]
+
+    def forward_low(t):
+        low = low_piece(t)
+        for d in range(4):
+
+            @pl.when(feeds[t][d])
+            def _():
+                remote(low, low, low_tree.at[t * 4 + d], low_recv.at[t], targets[d]).start()
+
+        remote(low, low, low_part.at[t], low_recv.at[t], partner).start()
+
     def forward_range(lo, hi):
         def one(c, carry):
             for t in range(TREES):
@@ -230,6 +251,13 @@
             return carry
 
         lax.fori_loop(lo, hi, one, 0)
+
+    @pl.when(is_root)
+    def _():
+        for piece in pieces[:TREES]:
+            piece.wait()
+        forward_range(0, per_piece)
+        find_sources()
 
     to_scalars.wait()
 
@@ -252,9 +280,6 @@
 
     @pl.when(is_root)
     def _():
-        for piece in pieces[:TREES]:
-            piece.wait()
-        forward_range(0, per_piece)
         for piece in pieces[TREES:]:
             piece.wait()
         gather_from(panel)
@@ -267,7 +292,7 @@
     d_copies = []
     for k in range(SIDE):
         where = (lax.rem(px + k, SIDE), pc + 1)
-        d_copies.append(remote(contrib, dbuf.at[px], d_send.at[k], d_recv.at[px], where))
+        d_copies.append(remote(contrib.at[pl.ds(0, NB)], dbuf.at[px], d_send.at[k], d_recv.at[px], where))
 
     @pl.when(is_root)
     def _():
@@ -295,6 +320,11 @@
         upper, urows = factors(inv[...], moved[pl.ds(0, NB), :])
         right_upper[...] = right_side(upper)
         right_rows[...] = right_side(urows)
+        solved[...] = urows
+
+    def make_fix():
+        low = product(low_rows[...], right_upper[...])
+        fix[...] = jnp.where(is_root, low, moved[pl.ds(NB, NB), :] - product(low, right_rows[...]))
 
     def update(starts, size):
         places = [pl.ds(pl.multiple_of(start, CHUNK), size) for start in starts]
@@ -312,28 +342,39 @@
             update_group(m * WIDE, WIDE)
             return carry
 
-        lax.fori_loop(lo // WIDE, hi // WIDE, one, 0)
+        lax.fori_loop(lax.div(lo, WIDE), hi // WIDE, one, 0)
 
     @pl.when(is_root)
     def _():
-        forward_range(per_piece, chunks)
+        low_at = min(LOW_AT, chunks - 1)
+        forward_range(per_piece, low_at)
         receive_moved()
-        arrived(packed, c_recv.at[1])
-        arrived(inv, c_recv.at[2])
+        low_rows[...] = moved[pl.ds(NB, NB), :]
+        for t in range(TREES):
+            forward_low(t)
+        forward_range(low_at, chunks)
+        arrived(packed, c_recv.at[0])
+        arrived(inv, c_recv.at[1])
         take_factors()
-        update_rest(0, chunks)
-
-    steps = chunks + max(max(lags(t)) for t in range(TREES))
-    ready = min(READY, steps)
-    done = min(steps - ready, chunks)
-    ready += done % WIDE
-    done -= done % WIDE
+        make_fix()
+        update_rest(jnp.int32(0), chunks)
+
+    assert (FASTER - READY) % WIDE == 0 and READY >= max(max(lags(t)) for t in range(TREES))
+    slow = min(FASTER - READY, chunks)
+    last = functools.reduce(jnp.maximum, delay) + chunks
+    pairs = lax.div(jnp.clip(last - FASTER, 0, (chunks - slow) // 2) + 1, 2) * 2
+    done = slow + 2 * pairs
 
     @pl.when(jnp.logical_and(core == 0, jnp.logical_not(is_root)))
     def _():
         def relay(i, carry):
             for t in range(TREES):
                 c = i - delay[t]
+
+                @pl.when(c == min(LOW_AT, chunks - 1))
+                def _():
+                    arrived(low_piece(t), low_recv.at[t])
+                    forward_low(t)
 
                 @pl.when(jnp.logical_and(c >= 0, c < chunks))
                 def _():
@@ -342,30 +383,32 @@
 
             return carry
 
-        def relay_and_update(i, carry):
+        def relay_and_one(i, carry):
             relay(i, carry)
-            update_group(i - ready, 1)
+            update_group(i - READY, 1)
             return carry
 
-        early = min(EARLY, ready)
-        lax.fori_loop(0, early, relay, 0)
+        def relay_and_two(i, carry):
+            relay(i, carry)
+            update_group(slow + (i - FASTER) * 2, 2)
+            return carry
+
+        lax.fori_loop(0, EARLY, relay, 0)
         receive_moved()
-        lax.fori_loop(early, ready, relay, 0)
-        arrived(packed, c_recv.at[1])
-        arrived(inv, c_recv.at[2])
+        lax.fori_loop(EARLY, READY, relay, 0)
+        arrived(packed, c_recv.at[0])
+        arrived(inv, c_recv.at[1])
         take_factors()
-        lax.fori_loop(ready, ready + done, relay_and_update, 0)
-        lax.fori_loop(ready + done, steps, relay, 0)
+        lax.fori_loop(READY, FASTER, relay_and_one, 0)
+        make_fix()
+        lax.fori_loop(FASTER, FASTER + pairs, relay_and_two, 0)
         update_rest(done, chunks)
 
-    z_copies = [remote(diag, diag, z_send.at[k], f_recv.at[0], z_peers[k]) for k in range(3)]
-    z_copies += [remote(low_rows, low_rows, z_send.at[3 + k], f_recv.at[1], z_peers[k]) for k in range(3)]
-    y_copies = [remote(diag, diag, y_send.at[k], f_recv.at[0], y_peers[k]) for k in range(3)]
-    y_copies += [remote(low_rows, low_rows, y_send.at[3 + k], f_recv.at[1], y_peers[k]) for k in range(3)]
+    z_copies = [remote(diag, diag, z_send.at[k], f_recv, z_peers[k]) for k in range(3)]
+    y_copies = [remote(diag, diag, y_send.at[k], f_recv, y_peers[k]) for k in range(3)]
     c_copies = [
-        remote(low_rows, low_rows, c_send.at[0], c_recv.at[0], partner),
-        remote(packed, packed, c_send.at[1], c_recv.at[1], partner),
-        remote(inv, inv, c_send.at[2], c_recv.at[2], partner),
+        remote(packed, packed, c_send.at[0], c_recv.at[0], partner),
+        remote(inv, inv, c_send.at[1], c_recv.at[1], partner),
     ]
 
     @pl.when(core == 1)
@@ -374,39 +417,24 @@
         def _():
             for k in range(SIDE):
                 arrived(dbuf.at[k], d_recv.at[k])
-            total = dbuf[0] + dbuf[1] + dbuf[2] + dbuf[3]
-            diag[...] = total[:NB]
-            low_rows[...] = total[NB:]
+            diag[...] = dbuf[0] + dbuf[1] + dbuf[2] + dbuf[3]
             for k in range(3):
                 z_copies[k].start()
             for k in range(3):
                 y_copies[k].start()
-            for k in range(3):
-                z_copies[3 + k].start()
-            for k in range(3):
-                y_copies[3 + k].start()
 
         @pl.when(jnp.logical_not(is_root1))
         def _():
-            arrived(diag, f_recv.at[0])
+            arrived(diag, f_recv)
 
             @pl.when(y == 0)
             def _():
                 for k in range(3):
                     y_copies[k].start()
-                arrived(low_rows, f_recv.at[1])
-                for k in range(3):
-                    y_copies[3 + k].start()
 
         packed[...] = diag[...]
         eliminate_and_invert(packed, inv)
         c_copies[1].start()
-        c_copies[2].start()
-
-        @pl.when(y != 0)
-        def _():
-            arrived(low_rows, f_recv.at[1])
-
         c_copies[0].start()
         receive_moved()
         take_factors()
@@ -418,7 +446,12 @@
             update_group(2 * m, 2)
             return carry
 
-        lax.fori_loop(0, chunks // 2, receive, 0)
+        late = chunks // 2 - chunks // 8
+        lax.fori_loop(0, late, receive, 0)
+        for t in range(TREES):
+            arrived(low_piece(t), low_recv.at[t])
+        make_fix()
+        lax.fori_loop(late, chunks // 2, receive, 0)
 
         for copy in c_copies:
             copy.wait_send()
@@ -435,7 +468,6 @@
 
     @pl.when(core == 0)
     def _():
-        arrived(low_rows, c_recv.at[0])
         for t in range(TREES):
             sent = panel.at[pl.ds(t * share, share)]
             for d in range(4):
@@ -445,20 +477,23 @@
                     remote(sent, sent, tree_sem.at[t * 4 + d], recv_sem.at[0], partner).wait_send()
 
             remote(sent, sent, part_sem.at[t], recv_sem.at[0], partner).wait_send()
+            low = low_piece(t)
+            for d in range(4):
+
+                @pl.when(feeds[t][d])
+                def _():
+                    remote(low, low, low_tree.at[t * 4 + d], low_recv.at[t], partner).wait_send()
+
+            remote(low, low, low_part.at[t], low_recv.at[t], partner).wait_send()
 
         @pl.when(is_root)
         def _():
             for copy in d_copies:
                 copy.wait_send()
 
-    low = product(low_rows[...], right_upper[...])
-    fix[...] = jnp.where(is_root, low, moved[pl.ds(NB, NB), :] - product(low, right_rows[...]))
-
     @pl.when(px == 0)
     def _():
-        lower = moved[pl.ds(0, NB), :]
-        urows = factors(inv[...], lower)[1]
-        held[pl.ds(0, NB), :] = jnp.where(is_root, packed[...], urows)
+        held[pl.ds(0, NB), :] = jnp.where(is_root, packed[...], solved[...])
 
     for copy in x_copies:
         copy.wait_send()
@@ -551,8 +586,9 @@
             pltpu.VMEM((rows_local, NB), F32),
             pltpu.VMEM((2 * NB, NB), F32),
             pltpu.VMEM((SIDE, 2 * NB, NB), F32),
-            pltpu.VMEM((SIDE, 2 * NB, NB), F32),
+            pltpu.VMEM((SIDE, NB, NB), F32),
             pltpu.VMEM((2 * NB, NB), F32),
+            square,
             square,
             square,
             square,
@@ -574,11 +610,14 @@
             dma((SIDE,)),
             dma((SIDE,)),
             dma((SIDE,)),
-            dma((6,)),
-            dma((6,)),
-            dma((2,)),
             dma((3,)),
             dma((3,)),
+            dma,
+            dma((2,)),
+            dma((2,)),
+            dma((TREES * 4,)),
+            dma((TREES,)),
+            dma((TREES,)),
         ],
         compiler_params=pltpu.CompilerParams(
             collective_id=0, has_side_effects=True, vmem_limit_bytes=VMEM_MIB * 2**20

time: 54.7 us -> 54.1 us (0.989)
  Pallas kernels: 54.2 us -> 53.3 us
    pallas_call x1, Pallas kernels: 49.7 us -> 48.8 us  [local(): pl.pallas_call(exchange_kernel, out_shape=(jax.ShapeDtypeStruct((rows_loc...]
where the time goes in v3:
time: 54.1 us; the launch traced here: 53.3 us
  Pallas kernels  53.3 us (99%)
    pallas_call x1, Pallas kernels, local(): pl.pallas_call(exchange_kernel, out_shape=(jax.ShapeDtypeStruct((rows_loc...  48.8 us
    pallas_call x1, Pallas kernels, local(): pl.pallas_call(finish_kernel, out_shape=jax.ShapeDtypeStruct((rows_local,...  4.56 us

profile of v3, /device:TPU:48, one launch (start us, length us, event | category | flops | bytes accessed | tf_op | source)
XLA Modules:
  0.0 53.3 jit_solution(8100495583202121913)
XLA Ops:
  0.0 0.0 copy-start
  0.0 48.8 %shard_map.28 = (f32[16384,128]{1,0:T(8,128)S(1)}, f32[128,128]{1,0:T(8,128)S(1)}) custom-call(s32[1,128]{1,0:T(1,128)} %bitcast.5, f32[16384,128]{1,0:T(8,128)} %bitcast.6), custom_call_target="tpu_custom_call" | custom-call | tf_op jit(solution)/shard_map/pallas_call | solution.py:577
  48.8 0.0 copy-done
  48.8 4.6 %shard_map.29 = f32[16384,128]{1,0:T(8,128)} custom-call(s32[128]{0:T(128)S(1)} %copy-done, f32[16384,128]{1,0:T(8,128)S(1)} %get-tuple-element.7.held, f32[128,128]{1,0:T(8,128)S(1)} %get-tuple-element.8.fix), custom_call_target="tpu_custom_call" | custom-call | tf_op jit(solution)/shard_map/pallas_call | solution.py:626
Async XLA Ops:
  0.0 48.8 %copy-start = (s32[128]{0:T(128)S(1)}, s32[128]{0:T(128)}, u32[]{:S(2)}) copy-start(s32[128]{0:T(128)} %piv_s.1) | copy-start | bytes 1540

commit v4 on v3

--- a/solution.py
+++ b/solution.py
@@ -23,7 +23,7 @@
 PLAIN, ROUND = 5, 6
 CHUNK = 128
 PIECES = 4
-EARLY = 24
+EARLY = 30
 LOW_AT = 16
 READY = 39
 FASTER = 47
@@ -261,22 +261,25 @@
 
     to_scalars.wait()
 
+    def gather(g, rows_ref):
+        for r in range(2):
+            base = pl.multiple_of(g * 8, 8)
+            found = []
+            for s in range(8):
+                source = src_s[r, g * 8 + s]
+                block = lax.div(source, NB)
+                mine = lax.rem(block, SIDE) == px
+                local = lax.div(block, SIDE) * NB + lax.rem(source, NB)
+                row = rows_ref[pl.ds(jnp.where(mine, local, 0), 1), :]
+                found.append(jnp.where(mine, row, 0.0))
+            contrib[pl.ds(r * NB + base, 8), :] = jnp.concatenate(found, axis=0)
+
     def gather_from(rows_ref):
-        def gather(g, carry):
-            for r in range(2):
-                base = pl.multiple_of(g * 8, 8)
-                found = []
-                for s in range(8):
-                    source = src_s[r, g * 8 + s]
-                    block = lax.div(source, NB)
-                    mine = lax.rem(block, SIDE) == px
-                    local = lax.div(block, SIDE) * NB + lax.rem(source, NB)
-                    row = rows_ref[pl.ds(jnp.where(mine, local, 0), 1), :]
-                    found.append(jnp.where(mine, row, 0.0))
-                contrib[pl.ds(r * NB + base, 8), :] = jnp.concatenate(found, axis=0)
-            return carry
-
-        lax.fori_loop(0, NB // 8, gather, 0)
+        def one(g, carry):
+            gather(g, rows_ref)
+            return carry
+
+        lax.fori_loop(0, NB // 8, one, 0)
 
     @pl.when(is_root)
     def _():
@@ -287,7 +290,10 @@
     @pl.when(jnp.logical_not(is_root))
     def _():
         hold.wait()
-        gather_from(held)
+
+        @pl.when(core == 1)
+        def _():
+            gather_from(held)
 
     d_copies = []
     for k in range(SIDE):
@@ -302,8 +308,11 @@
     x_copies = [
         remote(contrib, xbuf.at[px], x_send.at[k], x_recv.at[px], x_peers[k]) for k in range(SIDE - 1)
     ]
-    for copy in x_copies:
-        copy.start()
+
+    @pl.when(jnp.logical_or(core == 1, is_root))
+    def _():
+        for copy in x_copies:
+            copy.start()
 
     def arrived(ref, sem):
         pltpu.make_async_copy(ref, ref, sem).wait()
@@ -393,7 +402,15 @@
             update_group(slow + (i - FASTER) * 2, 2)
             return carry
 
-        lax.fori_loop(0, EARLY, relay, 0)
+        def relay_and_gather(i, carry):
+            relay(i, carry)
+            gather(i, held)
+            return carry
+
+        lax.fori_loop(0, NB // 8, relay_and_gather, 0)
+        for copy in x_copies:
+            copy.start()
+        lax.fori_loop(NB // 8, EARLY, relay, 0)
         receive_moved()
         lax.fori_loop(EARLY, READY, relay, 0)
         arrived(packed, c_recv.at[0])

time: 54.1 us -> 52.7 us (0.974)
  Pallas kernels: 53.3 us -> 52 us
    pallas_call x1, Pallas kernels: 48.8 us -> 47.4 us  [local(): pl.pallas_call(exchange_kernel, out_shape=(jax.ShapeDtypeStruct((rows_loc...]
where the time goes in v4:
time: 52.7 us; the launch traced here: 52 us
  Pallas kernels  52 us (99%)
    pallas_call x1, Pallas kernels, local(): pl.pallas_call(exchange_kernel, out_shape=(jax.ShapeDtypeStruct((rows_loc...  47.4 us
    pallas_call x1, Pallas kernels, local(): pl.pallas_call(finish_kernel, out_shape=jax.ShapeDtypeStruct((rows_local,...  4.62 us

profile of v4, /device:TPU:48, one launch (start us, length us, event | category | flops | bytes accessed | tf_op | source)
XLA Modules:
  0.0 52.0 jit_solution(16364288949449055554)
XLA Ops:
  0.0 0.0 copy-start
  0.0 47.4 %shard_map.28 = (f32[16384,128]{1,0:T(8,128)S(1)}, f32[128,128]{1,0:T(8,128)S(1)}) custom-call(s32[1,128]{1,0:T(1,128)} %bitcast.5, f32[16384,128]{1,0:T(8,128)} %bitcast.6), custom_call_target="tpu_custom_call" | custom-call | tf_op jit(solution)/shard_map/pallas_call | solution.py:594
  47.4 0.0 copy-done
  47.4 4.6 %shard_map.29 = f32[16384,128]{1,0:T(8,128)} custom-call(s32[128]{0:T(128)S(1)} %copy-done, f32[16384,128]{1,0:T(8,128)S(1)} %get-tuple-element.7.held, f32[128,128]{1,0:T(8,128)S(1)} %get-tuple-element.8.fix), custom_call_target="tpu_custom_call" | custom-call | tf_op jit(solution)/shard_map/pallas_call | solution.py:643
Async XLA Ops:
  0.0 47.4 %copy-start = (s32[128]{0:T(128)S(1)}, s32[128]{0:T(128)}, u32[]{:S(2)}) copy-start(s32[128]{0:T(128)} %piv_s.1) | copy-start | bytes 1540

commit v5 on v4

--- a/solution.py
+++ b/solution.py
@@ -23,8 +23,8 @@
 PLAIN, ROUND = 5, 6
 CHUNK = 128
 PIECES = 4
-EARLY = 30
-LOW_AT = 16
+EARLY = 32
+LOW_AT = 20
 READY = 39
 FASTER = 47
 WIDE = 4
@@ -259,7 +259,6 @@
         forward_range(0, per_piece)
         find_sources()
 
-    to_scalars.wait()
 
     def gather(g, rows_ref):
         for r in range(2):
@@ -285,15 +284,14 @@
     def _():
         for piece in pieces[TREES:]:
             piece.wait()
+        to_scalars.wait()
         gather_from(panel)
 
-    @pl.when(jnp.logical_not(is_root))
-    def _():
+    @pl.when(core == 1)
+    def _():
+        to_scalars.wait()
         hold.wait()
-
-        @pl.when(core == 1)
-        def _():
-            gather_from(held)
+        gather_from(held)
 
     d_copies = []
     for k in range(SIDE):
@@ -325,11 +323,17 @@
             total = total + xbuf[slot]
         moved[...] = total
 
+    def solve_rows():
+        solved[...] = factors(inv[...], moved[pl.ds(0, NB), :])[1]
+
+    def split_factors():
+        upper = factors(inv[...], moved[pl.ds(0, NB), :])[0]
+        right_upper[...] = right_side(upper)
+        right_rows[...] = right_side(solved[...])
+
     def take_factors():
-        upper, urows = factors(inv[...], moved[pl.ds(0, NB), :])
-        right_upper[...] = right_side(upper)
-        right_rows[...] = right_side(urows)
-        solved[...] = urows
+        solve_rows()
+        split_factors()
 
     def make_fix():
         low = product(low_rows[...], right_upper[...])
@@ -404,18 +408,24 @@
 
         def relay_and_gather(i, carry):
             relay(i, carry)
-            gather(i, held)
-            return carry
-
-        lax.fori_loop(0, NB // 8, relay_and_gather, 0)
+            gather(i - first, held)
+            return carry
+
+        first = PLAIN + 1
+        lax.fori_loop(0, first, relay, 0)
+        to_scalars.wait()
+        hold.wait()
+        lax.fori_loop(first, first + NB // 8, relay_and_gather, 0)
         for copy in x_copies:
             copy.start()
-        lax.fori_loop(NB // 8, EARLY, relay, 0)
+        lax.fori_loop(first + NB // 8, EARLY, relay, 0)
         receive_moved()
-        lax.fori_loop(EARLY, READY, relay, 0)
+        lax.fori_loop(EARLY, READY - 1, relay, 0)
         arrived(packed, c_recv.at[0])
         arrived(inv, c_recv.at[1])
-        take_factors()
+        solve_rows()
+        lax.fori_loop(READY - 1, READY, relay, 0)
+        split_factors()
         lax.fori_loop(READY, FASTER, relay_and_one, 0)
         make_fix()
         lax.fori_loop(FASTER, FASTER + pairs, relay_and_two, 0)
@@ -468,7 +478,14 @@
         for t in range(TREES):
             arrived(low_piece(t), low_recv.at[t])
         make_fix()
-        lax.fori_loop(late, chunks // 2, receive, 0)
+        def receive_one(i, carry):
+            for t in range(TREES):
+                arrived(chunk_at(t, i), recv_sem.at[t * chunks + i])
+            update_group(i, 1)
+            return carry
+
+        lax.fori_loop(late, chunks // 2 - 1, receive, 0)
+        lax.fori_loop(chunks - 2, chunks, receive_one, 0)
 
         for copy in c_copies:
             copy.wait_send()

time: 52.7 us -> 52.4 us (level)
  no operation moved by 1% of the time
where the time goes in v5:
time: 52.4 us; the launch traced here: 51.7 us
  Pallas kernels  51.7 us (99%)
    pallas_call x1, Pallas kernels, local(): pl.pallas_call(exchange_kernel, out_shape=(jax.ShapeDtypeStruct((rows_loc...  47.2 us
    pallas_call x1, Pallas kernels, local(): pl.pallas_call(finish_kernel, out_shape=jax.ShapeDtypeStruct((rows_local,...  4.53 us

profile of v5, /device:TPU:48, one launch (start us, length us, event | category | flops | bytes accessed | tf_op | source)
XLA Modules:
  0.0 51.7 jit_solution(15080323280704681302)
XLA Ops:
  0.0 0.0 copy-start
  0.0 47.2 %shard_map.28 = (f32[16384,128]{1,0:T(8,128)S(1)}, f32[128,128]{1,0:T(8,128)S(1)}) custom-call(s32[1,128]{1,0:T(1,128)} %bitcast.5, f32[16384,128]{1,0:T(8,128)} %bitcast.6), custom_call_target="tpu_custom_call" | custom-call | tf_op jit(solution)/shard_map/pallas_call | solution.py:611
  47.2 0.0 copy-done
  47.2 4.5 %shard_map.29 = f32[16384,128]{1,0:T(8,128)} custom-call(s32[128]{0:T(128)S(1)} %copy-done, f32[16384,128]{1,0:T(8,128)S(1)} %get-tuple-element.7.held, f32[128,128]{1,0:T(8,128)S(1)} %get-tuple-element.8.fix), custom_call_target="tpu_custom_call" | custom-call | tf_op jit(solution)/shard_map/pallas_call | solution.py:660
Async XLA Ops:
  0.0 47.2 %copy-start = (s32[128]{0:T(128)S(1)}, s32[128]{0:T(128)}, u32[]{:S(2)}) copy-start(s32[128]{0:T(128)} %piv_s.1) | copy-start | bytes 1540

commit v6 on v5

--- a/solution.py
+++ b/solution.py
@@ -26,7 +26,7 @@
 EARLY = 32
 LOW_AT = 20
 READY = 39
-FASTER = 47
+FASTER = 51
 WIDE = 4
 VMEM_MIB = 40
 

time: 52.4 us -> 52.4 us (level)
  no operation moved by 1% of the time
where the time goes in v6:
time: 52.4 us; the launch traced here: 52.2 us
  Pallas kernels  52.2 us (100%)
    pallas_call x1, Pallas kernels, local(): pl.pallas_call(exchange_kernel, out_shape=(jax.ShapeDtypeStruct((rows_loc...  47.6 us
    pallas_call x1, Pallas kernels, local(): pl.pallas_call(finish_kernel, out_shape=jax.ShapeDtypeStruct((rows_local,...  4.56 us

profile of v6, /device:TPU:48, one launch (start us, length us, event | category | flops | bytes accessed | tf_op | source)
XLA Modules:
  0.0 52.2 jit_solution(7874880362221697692)
XLA Ops:
  0.0 0.0 copy-start
  0.0 47.6 %shard_map.28 = (f32[16384,128]{1,0:T(8,128)S(1)}, f32[128,128]{1,0:T(8,128)S(1)}) custom-call(s32[1,128]{1,0:T(1,128)} %bitcast.5, f32[16384,128]{1,0:T(8,128)} %bitcast.6), custom_call_target="tpu_custom_call" | custom-call | tf_op jit(solution)/shard_map/pallas_call | solution.py:611
  47.7 0.0 copy-done
  47.7 4.6 %shard_map.29 = f32[16384,128]{1,0:T(8,128)} custom-call(s32[128]{0:T(128)S(1)} %copy-done, f32[16384,128]{1,0:T(8,128)S(1)} %get-tuple-element.7.held, f32[128,128]{1,0:T(8,128)S(1)} %get-tuple-element.8.fix), custom_call_target="tpu_custom_call" | custom-call | tf_op jit(solution)/shard_map/pallas_call | solution.py:660
Async XLA Ops:
  0.0 47.7 %copy-start = (s32[128]{0:T(128)S(1)}, s32[128]{0:T(128)}, u32[]{:S(2)}) copy-start(s32[128]{0:T(128)} %piv_s.1) | copy-start | bytes 1540
